TPU v7x, 512 devices: a whole 4x4x16 slice. The times are simulated.
512 devices in a mesh: seq: 32 (over y, x, core), tp: 16 (over z).
Axes of the slice: x: 4, y: 4, z: 16, core: 2. Of those that a mesh axis runs over, the one named last changes fastest.
Arguments:
- tokens: bfloat16 [4096, 4096], P('seq', 'tp'), may hold values from -6 to 6
- in_weight: bfloat16 [4096, 8192], P(None, 'tp'), may hold values from -0.09375 to 0.09375
- conv_weight: float32 [4, 8192], P(None, 'tp'), may hold values from -3 to 3
- conv_bias: float32 [8192], P('tp'), may hold values from -0.5 to 0.5
- proj_weight: bfloat16 [8192, 288], P('tp'), may hold values from -0.0625 to 0.0625
- dt_weight: bfloat16 [256, 8192], P(None, 'tp'), may hold values from -0.375 to 0.375
- dt_bias: float32 [8192], P('tp'), may hold values from -7 to -2
- a_log: float32 [16, 8192], P(None, 'tp'), may hold values from -3 to 1.5
- skip_gain: float32 [8192], P('tp'), may hold values from 0.5 to 1.5
- threshold: float32 [8192], P('tp'), may hold values from -0.5 to 0.5
Outputs:
- gated: bfloat16 [4096, 8192], P('seq', 'tp')
All inputs are finite; a program needn't handle non-finite values.
Results may differ from a plain program's by a relative error of at most 0.0085.
Values may be sent and summed in bfloat16 or wider, within the bound.
No kernel may reach another device: no remote copies, remote signals or barrier semaphores. Data moves between devices by JAX's collectives and lax.ppermute only.
A program may use at most 64 MiB of HBM per device.

v0:
```python
import math
import jax
import jax.numpy as jnp
from jax import lax
from jax.sharding import PartitionSpec as P


def shifted(x, axis, by):
    peers = lax.axis_size(axis)
    pairs = [(i, i + by) for i in range(peers) if 0 <= i + by < peers]
    return lax.ppermute(x, axis, pairs)


def carried_in(value, axis, join, neutral):
    count, mine = (lax.axis_size(axis), lax.axis_index(axis))
    pieces = jax.tree.map(lambda part: lax.all_gather(part, axis), value)
    total = jax.tree.map(
        lambda part, zero: jnp.full_like(part, 0) + jnp.asarray(zero, part.dtype), value, neutral
    )

    def turn(position, total):
        longer = join(total, jax.tree.map(lambda part: part[position], pieces))
        return jax.tree.map(lambda new, old: jnp.where(position < mine, new, old), longer, total)

    return lax.fori_loop(0, count - 1, turn, total)


def combine_pair(earlier, later):
    return (earlier[0] * later[0], later[0] * earlier[1] + later[1])


def lower_table(rows):
    row_ids = lax.broadcasted_iota(jnp.int32, (rows, rows), 0)
    col_ids = lax.broadcasted_iota(jnp.int32, (rows, rows), 1)
    return row_ids >= col_ids


def local_pass(step_size, inflow_rows, b_coef, c_coef, rate, start_state, block):
    rows, width = step_size.shape
    count = rows // block
    lower = lower_table(block)
    lower_float = lower.astype(jnp.float32)

    def run(carry, items):
        state, decay_all = carry
        step_block, flow_block, b_block, c_block = items
        summed = jnp.dot(
            lower_float,
            step_block,
            precision=lax.Precision.HIGHEST,
            preferred_element_type=jnp.float32,
        )
        diff = jnp.where(lower[:, :, None], summed[:, None, :] - summed[None, :, :], 0.0)
        weights = jnp.where(
            lower[:, :, None, None], jnp.exp(diff[:, :, None, :] * rate[None, None]), 0.0
        )
        inflow = flow_block[:, None, :] * b_block[:, :, None]
        states = jnp.einsum("tsnc,snc->tnc", weights, inflow, precision=lax.Precision.HIGHEST)
        states = states + jnp.exp(summed[:, None, :] * rate[None]) * state[None]
        outputs = jnp.einsum("tn,tnc->tc", c_block, states, precision=lax.Precision.HIGHEST)
        block_decay = jnp.exp(summed[-1][None, :] * rate)
        return ((states[-1], block_decay * decay_all), outputs)

    items = (
        step_size.reshape(count, block, width),
        inflow_rows.reshape(count, block, width),
        b_coef.reshape(count, block, -1),
        c_coef.reshape(count, block, -1),
    )
    (end_state, decay_all), outputs = lax.scan(
        run, (start_state, jnp.ones_like(start_state)), items
    )
    return (end_state, decay_all, outputs.reshape(rows, width))


def per_device(
    tokens,
    in_weight,
    conv_weight,
    conv_bias,
    proj_weight,
    dt_weight,
    dt_bias,
    a_log,
    skip_gain,
    threshold,
):
    tok_rows = tokens.shape[0]
    width = in_weight.shape[1]
    taps = conv_weight.shape[0]
    rank = dt_weight.shape[0]
    states_n = a_log.shape[0]
    projected = jnp.dot(
        lax.all_gather(tokens, "tp", axis=1, tiled=True),
        in_weight,
        preferred_element_type=jnp.float32,
    ).astype(jnp.bfloat16)
    rim_inner = shifted(projected[tok_rows - taps + 1 :], "seq", 1)
    padded = jnp.concatenate([rim_inner, projected], axis=0)
    pre = conv_bias[None, :] + jnp.zeros((tok_rows, width), jnp.float32)
    for k in range(taps):
        pre = pre + conv_weight[k][None, :] * padded[k : k + tok_rows].astype(jnp.float32)
    u_half = jax.nn.silu(pre).astype(jnp.bfloat16)
    partial_sums = jnp.dot(u_half, proj_weight, preferred_element_type=jnp.float32)
    total = lax.psum(partial_sums, "tp")
    dt_low = total[:, :rank].astype(jnp.bfloat16)
    b_coef = total[:, rank : rank + states_n]
    c_coef = total[:, rank + states_n :]
    step_size = jax.nn.softplus(
        jnp.dot(dt_low, dt_weight, preferred_element_type=jnp.float32) + dt_bias[None, :]
    )
    rate = -jnp.exp(a_log)
    u_float = u_half.astype(jnp.float32)
    inflow_rows = step_size * u_float
    block = math.gcd(tok_rows, 16)
    zero_state = jnp.zeros((states_n, width), jnp.float32)
    end_state, decay_all, local_out = local_pass(
        step_size, inflow_rows, b_coef, c_coef, rate, zero_state, block
    )
    incoming = carried_in(
        (decay_all, end_state), "seq", combine_pair, (jnp.ones_like(decay_all), zero_state)
    )
    entry_state = incoming[1]
    whole_lower = lower_table(tok_rows).astype(jnp.float32)
    summed = jnp.dot(
        whole_lower, step_size, precision=lax.Precision.HIGHEST, preferred_element_type=jnp.float32
    )
    growth = jnp.exp(summed[:, None, :] * rate[None])
    scan_out = local_out + jnp.einsum(
        "tn,tnc->tc", c_coef, growth * entry_state[None], precision=lax.Precision.HIGHEST
    )
    y_full = scan_out + skip_gain[None, :] * u_float
    return (y_full * jax.nn.sigmoid(4.0 * (y_full - threshold[None, :]))).astype(jnp.bfloat16)


def solution(mesh):
    return jax.shard_map(
        per_device,
        mesh=mesh,
        in_specs=(
            P("seq", "tp"),
            P(None, "tp"),
            P(None, "tp"),
            P("tp"),
            P("tp", None),
            P(None, "tp"),
            P("tp"),
            P(None, "tp"),
            P("tp"),
            P("tp"),
        ),
        out_specs=P("seq", "tp"),
        check_vma=False,
    )
```

profile of v0, /device:TPU:1, one launch (start us, length us, event | category | flops | bytes accessed | tf_op | source)
XLA Modules:
  0.0 405.8 jit_solution(9924214870880622098)
XLA Ops:
  7.3 68.5 %all-gather.6.cloned.1.call-done = bf16[128,4096]{1,0:T(8,128)(2,1)} async-done(((bf16[128,256]{1,0:T(8,128)(2,1)}), bf16[128,4096]{1,0:T(8,128)(2,1)}) %all-gather.6.cloned.1.call-update) | async-done | bytes 1048592 | tf_op jit(solution)/shard_map/all_gather | solution.py:94
  75.8 3.2 convolution_convert_fusion
  79.1 14.8 %collective-permute-start = (bf16[3,512]{1,0:T(4,128)(2,1)S(1)}, bf16[3,512]{1,0:T(4,128)(2,1)S(1)}, u32[]{:S(2)}, u32[]{:S(2)}) collective-permute-start(bf16[3,512]{1,0:T(4,128)(2,1)S(1)} %slice.57), channel_id=1, source_target_pairs={{0,16},{16,32},{32,48},{48,64},{64,80},{80,96},{96,112},{112,128},... | collective-permute-start | bytes 9224 | tf_op jit(solution)/shard_map/ppermute | solution.py:11
  94.9 0.9 fusion.23
  95.9 121.1 %all-reduce.2.cloned.1.call-done = f32[128,288]{0,1:T(8,128)} async-done(((f32[128,288]{0,1:T(8,128)}), f32[128,288]{0,1:T(8,128)}) %all-reduce.2.cloned.1.call-update) | async-done | bytes 147472 | tf_op jit(solution)/shard_map/psum | solution.py:105
  217.9 1.3 convert_multiply_fusion.1
  219.1 25.1 %while.31 = (s32[]{:T(128)}, f32[16,512]{1,0:T(8,128)S(1)}, f32[16,512]{1,0:T(8,128)S(1)}, f32[8,16,512]{2,1,0:T(8,128)S(1)}, f32[8,16,512]{2,1,0:T(8,128)S(1)},...) while((s32[]{:T(128)}, f32[16,512]{1,0:T(8,128)S(1)}, ...), condition=%wide.region_2.3_spmd.clone.clone, body=%wide.region_1.2_spmd.clone.clone.sunk | while | flops 12215043 | bytes 4797323 | solution.py:70
  219.5 2.2 multiply_reduce_fusion.2
  222.7 2.2 multiply_reduce_fusion.2
  225.8 2.2 multiply_reduce_fusion.2
  228.9 2.2 multiply_reduce_fusion.2
  232.1 2.2 multiply_reduce_fusion.2
  235.2 2.2 multiply_reduce_fusion.2
  238.3 2.2 multiply_reduce_fusion.2
  241.5 2.2 multiply_reduce_fusion.2
  245.9 63.7 %all-gather.8.cloned.1.call-done = f32[512,512]{1,0:T(8,128)} async-done(((f32[16,512]{1,0:T(8,128)}), f32[512,512]{1,0:T(8,128)}) %all-gather.8.cloned.1.call-update) | async-done | bytes 1048592 | tf_op jit(solution)/shard_map/all_gather | solution.py:16
  309.6 61.0 %all-gather.10.cloned.1.call-done = f32[512,512]{1,0:T(8,128)} async-done(((f32[16,512]{1,0:T(8,128)}), f32[512,512]{1,0:T(8,128)}) %all-gather.10.cloned.1.call-update) | async-done | bytes 1048592 | tf_op jit(solution)/shard_map/all_gather | solution.py:16
  370.6 25.2 %while.30 = (s32[]{:T(128)}, f32[16,512]{1,0:T(8,128)S(1)}, s32[]{:T(128)}, f32[32,16,512]{2,1,0:T(8,128)}, f32[32,16,512]{2,1,0:T(8,128)}, /*index=5*/s32[]{:T(128)}, s32[]{:T(128)}) while((s32[]{:T(128)}, f32[16,512]{1,0:T(8,128)S(1)}, s32[]{:T(128)}, f32[32,16,512]{2,1,0:T(8,128)}, f32[32,16,512]{2,1,0:T(8,128)}, ...), condition=%wide.region_4.5_spmd.clone, body=%wide.region_3.4_spmd.clone.sunk | while | flops 32772 | bytes 131173 | solution.py:25
  375.5 0.8 fusion.39
  376.3 0.8 fusion.39
  377.1 0.8 fusion.39
  377.9 0.8 fusion.39
  383.6 0.8 fusion.39
  395.8 2.7 fusion.9
  (165 shorter events, 32.3 us)
Async XLA Ops:
  6.5 88.3 %copy-start = (bf16[512,288]{0,1:T(8,128)(2,1)S(1)}, bf16[512,288]{0,1:T(8,128)(2,1)}, u32[]{:S(2)}) copy-start(bf16[512,288]{0,1:T(8,128)(2,1)} %param.18) | copy-start | bytes 884740
  6.5 87.4 %copy-start.5 = (f32[4,512]{1,0:T(4,128)S(1)}, f32[4,512]{1,0:T(4,128)}, u32[]{:S(2)}) copy-start(f32[4,512]{1,0:T(4,128)} %param.16) | copy-start | bytes 24580
  6.5 88.1 %copy-start.6 = (f32[512]{0:T(512)S(1)}, f32[512]{0:T(512)}, u32[]{:S(2)}) copy-start(f32[512]{0:T(512)} %param.17) | copy-start | bytes 6148
  6.5 89.3 %copy-start.4 = (f32[16,512]{1,0:T(8,128)S(1)}, f32[16,512]{1,0:T(8,128)}, u32[]{:S(2)}) copy-start(f32[16,512]{1,0:T(8,128)} %param.21) | copy-start | bytes 98308
  6.5 211.3 %copy-start.3 = (bf16[256,512]{1,0:T(8,128)(2,1)S(1)}, bf16[256,512]{1,0:T(8,128)(2,1)}, u32[]{:S(2)}) copy-start(bf16[256,512]{1,0:T(8,128)(2,1)} %param.19) | copy-start | bytes 786436
  6.5 211.3 %copy-start.7 = (f32[512]{0:T(512)S(1)}, f32[512]{0:T(512)}, u32[]{:S(2)}) copy-start(f32[512]{0:T(512)} %param.20) | copy-start | bytes 6148
  6.6 69.3 %all-gather.6.cloned.1.call-start = ((), (), s32[]{:S(2)}) async-start(), calls=%async_computation | async-start | bytes 1114112 | tf_op jit(solution)/shard_map/all_gather | solution.py:94
  7.3 209.6 %all-reduce.2.cloned.1.call-start = ((), (), s32[]{:S(2)}) async-start(), calls=%async_computation.1 | async-start | bytes 294912 | tf_op jit(solution)/shard_map/psum | solution.py:105
  79.1 15.6 %collective-permute-start = (bf16[3,512]{1,0:T(4,128)(2,1)S(1)}, bf16[3,512]{1,0:T(4,128)(2,1)S(1)}, u32[]{:S(2)}, u32[]{:S(2)}) collective-permute-start(bf16[3,512]{1,0:T(4,128)(2,1)S(1)} %slice.57), channel_id=1, source_target_pairs={{0,16},{16,32},{32,48},{48,64},{64,80},{80,96},{96,112},{112,128},... | collective-permute-start | bytes 9224 | tf_op jit(solution)/shard_map/ppermute | solution.py:11
  95.8 213.8 %all-gather.8.cloned.1.call-start = ((), (), s32[]{:S(2)}) async-start(), calls=%async_computation.2 | async-start | bytes 1081344 | tf_op jit(solution)/shard_map/all_gather | solution.py:16
  244.2 0.6 copy-start.2
  244.2 0.7 copy-start.1
  244.2 154.3 %copy-start.8 = (f32[512]{0:T(512)S(1)}, f32[512]{0:T(512)}, u32[]{:S(2)}) copy-start(f32[512]{0:T(512)} %param.23) | copy-start | bytes 6148
  244.3 154.3 %copy-start.9 = (f32[512]{0:T(512)S(1)}, f32[512]{0:T(512)}, u32[]{:S(2)}) copy-start(f32[512]{0:T(512)} %param.22) | copy-start | bytes 6148
  244.9 125.8 %all-gather.10.cloned.1.call-start = ((), (), s32[]{:S(2)}) async-start(), calls=%async_computation.3 | async-start | bytes 1081344 | tf_op jit(solution)/shard_map/all_gather | solution.py:16
Sparse Core Ops, SparseCore 0:
  9.4 66.3 all-gather.5
  95.9 120.9 all-reduce.1
  245.0 64.5 all-gather.7
  313.1 57.5 all-gather.9
where the time goes:
time: 408 us; the launch traced here: 406 us
  waiting for transfers between devices  316 us (77%)
  other arithmetic  44.8 us (11%)
  starting transfers between devices  15 us (4%)
  between operations  13.4 us (3%)
  matrix products  12.7 us (3%)
    all_gather x2, waiting for transfers between devices, carried_in(): pieces = jax.tree.map(lambda part: lax.all_gather(part, axis), value)  125 us
    psum x1, waiting for transfers between devices, per_device(): total = lax.psum(partial_sums, 'tp')  121 us
    all_gather x1, waiting for transfers between devices, per_device(): lax.all_gather(tokens, 'tp', axis=1, tiled=True)  68.5 us
    select_n x31, other arithmetic, turn(): jnp.where(position < mine, new, old)  24.5 us
    dot_general x8, other arithmetic, run(): jnp.einsum('tsnc,snc->tnc', weights, inflow, precision=lax.Precision.HIGH...  17.3 us
    ppermute x1, starting transfers between devices, shifted(): return lax.ppermute(x, axis, pairs)  14.8 us
  transfers between devices with their start and end apart: 5, of which 5 were waited for; matrix products, arithmetic and copies ran while one was open for 0% of the time, Pallas kernels for 0%

commit v1 on v0

--- a/solution.py
+++ b/solution.py
@@ -3,6 +3,11 @@
 import jax.numpy as jnp
 from jax import lax
 from jax.sharding import PartitionSpec as P
+
+
+def summed_here(x, mesh_axis):
+    parts = lax.all_gather(x, mesh_axis)
+    return jnp.sum(parts, axis=0)
 
 
 def shifted(x, axis, by):
@@ -102,7 +107,7 @@
         pre = pre + conv_weight[k][None, :] * padded[k : k + tok_rows].astype(jnp.float32)
     u_half = jax.nn.silu(pre).astype(jnp.bfloat16)
     partial_sums = jnp.dot(u_half, proj_weight, preferred_element_type=jnp.float32)
-    total = lax.psum(partial_sums, "tp")
+    total = summed_here(partial_sums, "tp")
     dt_low = total[:, :rank].astype(jnp.bfloat16)
     b_coef = total[:, rank : rank + states_n]
     c_coef = total[:, rank + states_n :]

time: 408 us -> 355 us (0.87)
  waiting for transfers between devices: 316 us -> 262 us
    psum x1 -> x0, waiting for transfers between devices: 121 us -> none  [per_device(): total = lax.psum(partial_sums, 'tp')]
    all_gather x0 -> x1, waiting for transfers between devices: none -> 67.6 us  [summed_here(): parts = lax.all_gather(x, mesh_axis)]
where the time goes in v1:
time: 355 us; the launch traced here: 353 us
  waiting for transfers between devices  262 us (74%)
  other arithmetic  45.3 us (13%)
  starting transfers between devices  15 us (4%)
  between operations  13.4 us (4%)
  matrix products  11.8 us (3%)
    all_gather x2, waiting for transfers between devices, carried_in(): pieces = jax.tree.map(lambda part: lax.all_gather(part, axis), value)  124 us
    all_gather x1, waiting for transfers between devices, per_device(): lax.all_gather(tokens, 'tp', axis=1, tiled=True)  68.5 us
    all_gather x1, waiting for transfers between devices, summed_here(): parts = lax.all_gather(x, mesh_axis)  67.6 us
    select_n x31, other arithmetic, turn(): jnp.where(position < mine, new, old)  24.5 us
    dot_general x8, other arithmetic, run(): jnp.einsum('tsnc,snc->tnc', weights, inflow, precision=lax.Precision.HIGH...  17.3 us
    ppermute x1, starting transfers between devices, shifted(): return lax.ppermute(x, axis, pairs)  14.8 us
  transfers between devices with their start and end apart: 5, of which 5 were waited for; matrix products, arithmetic and copies ran while one was open for 0% of the time, Pallas kernels for 0%

profile of v1, /device:TPU:1, one launch (start us, length us, event | category | flops | bytes accessed | tf_op | source)
XLA Modules:
  0.0 352.5 jit_solution(10806335675563479926)
XLA Ops:
  7.3 68.5 %all-gather.8.cloned.1.call-done = bf16[128,4096]{1,0:T(8,128)(2,1)} async-done(((bf16[128,256]{1,0:T(8,128)(2,1)}), bf16[128,4096]{1,0:T(8,128)(2,1)}) %all-gather.8.cloned.1.call-update) | async-done | bytes 1048592 | tf_op jit(solution)/shard_map/all_gather | solution.py:99
  75.8 3.2 convolution_convert_fusion
  79.1 14.8 %collective-permute-start = (bf16[3,512]{1,0:T(4,128)(2,1)S(1)}, bf16[3,512]{1,0:T(4,128)(2,1)S(1)}, u32[]{:S(2)}, u32[]{:S(2)}) collective-permute-start(bf16[3,512]{1,0:T(4,128)(2,1)S(1)} %slice.57), channel_id=1, source_target_pairs={{0,16},{16,32},{32,48},{48,64},{64,80},{80,96},{96,112},{112,128},... | collective-permute-start | bytes 9224 | tf_op jit(solution)/shard_map/ppermute | solution.py:16
  94.8 0.9 fusion.23
  95.9 67.6 %all-gather.10.cloned.1.call-done = f32[2048,288]{0,1:T(8,128)} async-done(((f32[128,288]{0,1:T(8,128)}), f32[2048,288]{0,1:T(8,128)}) %all-gather.10.cloned.1.call-update) | async-done | bytes 2359312 | tf_op jit(solution)/shard_map/all_gather | solution.py:9
  163.5 2.1 copy.27
  166.6 25.1 %while.31 = (s32[]{:T(128)}, f32[16,512]{1,0:T(8,128)S(1)}, f32[16,512]{1,0:T(8,128)S(1)}, f32[8,16,512]{2,1,0:T(8,128)S(1)}, f32[8,16,512]{2,1,0:T(8,128)S(1)},...) while((s32[]{:T(128)}, f32[16,512]{1,0:T(8,128)S(1)}, ...), condition=%wide.region_2.3_spmd.clone.clone, body=%wide.region_1.2_spmd.clone.clone.sunk | while | flops 12215043 | bytes 4797323 | solution.py:75
  167.0 2.2 multiply_reduce_fusion.2
  170.1 2.2 multiply_reduce_fusion.2
  173.3 2.2 multiply_reduce_fusion.2
  176.4 2.2 multiply_reduce_fusion.2
  179.5 2.2 multiply_reduce_fusion.2
  182.7 2.2 multiply_reduce_fusion.2
  185.8 2.2 multiply_reduce_fusion.2
  188.9 2.2 multiply_reduce_fusion.2
  193.3 63.4 %all-gather.12.cloned.1.call-done = f32[512,512]{1,0:T(8,128)} async-done(((f32[16,512]{1,0:T(8,128)}), f32[512,512]{1,0:T(8,128)}) %all-gather.12.cloned.1.call-update) | async-done | bytes 1048592 | tf_op jit(solution)/shard_map/all_gather | solution.py:21
  256.7 60.5 %all-gather.14.cloned.1.call-done = f32[512,512]{1,0:T(8,128)} async-done(((f32[16,512]{1,0:T(8,128)}), f32[512,512]{1,0:T(8,128)}) %all-gather.14.cloned.1.call-update) | async-done | bytes 1048592 | tf_op jit(solution)/shard_map/all_gather | solution.py:21
  317.2 25.3 %while.30 = (s32[]{:T(128)}, f32[16,512]{1,0:T(8,128)S(1)}, s32[]{:T(128)}, f32[32,16,512]{2,1,0:T(8,128)}, f32[32,16,512]{2,1,0:T(8,128)}, /*index=5*/s32[]{:T(128)}, s32[]{:T(128)}) while((s32[]{:T(128)}, f32[16,512]{1,0:T(8,128)S(1)}, s32[]{:T(128)}, f32[32,16,512]{2,1,0:T(8,128)}, f32[32,16,512]{2,1,0:T(8,128)}, ...), condition=%wide.region_4.5_spmd.clone, body=%wide.region_3.4_spmd.clone.sunk | while | flops 32772 | bytes 131173 | solution.py:30
  318.0 0.8 fusion.39
  318.8 0.8 fusion.39
  319.7 0.8 fusion.39
  320.5 0.8 fusion.39
  321.3 0.8 fusion.39
  342.5 2.7 fusion.9
  (167 shorter events, 32.4 us)
Async XLA Ops:
  6.5 88.3 %copy-start = (bf16[512,288]{0,1:T(8,128)(2,1)S(1)}, bf16[512,288]{0,1:T(8,128)(2,1)}, u32[]{:S(2)}) copy-start(bf16[512,288]{0,1:T(8,128)(2,1)} %param.18) | copy-start | bytes 884740
  6.5 87.4 %copy-start.5 = (f32[4,512]{1,0:T(4,128)S(1)}, f32[4,512]{1,0:T(4,128)}, u32[]{:S(2)}) copy-start(f32[4,512]{1,0:T(4,128)} %param.16) | copy-start | bytes 24580
  6.5 88.1 %copy-start.6 = (f32[512]{0:T(512)S(1)}, f32[512]{0:T(512)}, u32[]{:S(2)}) copy-start(f32[512]{0:T(512)} %param.17) | copy-start | bytes 6148
  6.5 89.3 %copy-start.4 = (f32[16,512]{1,0:T(8,128)S(1)}, f32[16,512]{1,0:T(8,128)}, u32[]{:S(2)}) copy-start(f32[16,512]{1,0:T(8,128)} %param.21) | copy-start | bytes 98308
  6.5 69.3 %all-gather.8.cloned.1.call-start = ((), (), s32[]{:S(2)}) async-start(), calls=%async_computation | async-start | bytes 1114112 | tf_op jit(solution)/shard_map/all_gather | solution.py:99
  7.3 156.2 %all-gather.10.cloned.1.call-start = ((), (), s32[]{:S(2)}) async-start(), calls=%async_computation.1 | async-start | bytes 2506752 | tf_op jit(solution)/shard_map/all_gather | solution.py:9
  79.1 15.6 %collective-permute-start = (bf16[3,512]{1,0:T(4,128)(2,1)S(1)}, bf16[3,512]{1,0:T(4,128)(2,1)S(1)}, u32[]{:S(2)}, u32[]{:S(2)}) collective-permute-start(bf16[3,512]{1,0:T(4,128)(2,1)S(1)} %slice.57), channel_id=1, source_target_pairs={{0,16},{16,32},{32,48},{48,64},{64,80},{80,96},{96,112},{112,128},... | collective-permute-start | bytes 9224 | tf_op jit(solution)/shard_map/ppermute | solution.py:16
  94.6 71.6 %copy-start.3 = (bf16[256,512]{1,0:T(8,128)(2,1)S(1)}, bf16[256,512]{1,0:T(8,128)(2,1)}, u32[]{:S(2)}) copy-start(bf16[256,512]{1,0:T(8,128)(2,1)} %param.19) | copy-start | bytes 786436
  94.6 71.6 %copy-start.7 = (f32[512]{0:T(512)S(1)}, f32[512]{0:T(512)}, u32[]{:S(2)}) copy-start(f32[512]{0:T(512)} %param.20) | copy-start | bytes 6148
  95.8 160.9 %all-gather.12.cloned.1.call-start = ((), (), s32[]{:S(2)}) async-start(), calls=%async_computation.2 | async-start | bytes 1081344 | tf_op jit(solution)/shard_map/all_gather | solution.py:21
  191.7 0.6 copy-start.2
  191.7 0.7 copy-start.1
  191.7 153.5 %copy-start.8 = (f32[512]{0:T(512)S(1)}, f32[512]{0:T(512)}, u32[]{:S(2)}) copy-start(f32[512]{0:T(512)} %param.23) | copy-start | bytes 6148
  191.7 153.5 %copy-start.9 = (f32[512]{0:T(512)S(1)}, f32[512]{0:T(512)}, u32[]{:S(2)}) copy-start(f32[512]{0:T(512)} %param.22) | copy-start | bytes 6148
  192.3 124.9 %all-gather.14.cloned.1.call-start = ((), (), s32[]{:S(2)}) async-start(), calls=%async_computation.3 | async-start | bytes 1081344 | tf_op jit(solution)/shard_map/all_gather | solution.py:21
Sparse Core Ops, SparseCore 0:
  9.4 66.3 all-gather.7
  95.9 67.5 all-gather.9
  192.4 64.1 all-gather.11
  259.7 57.5 all-gather.13
